TPU v7x, 32 devices: a whole 2x2x4 slice. The times are simulated.
32 devices in a mesh: dp: 2 (over x), row: 4 (over y, core), col: 4 (over z).
Axes of the slice: x: 2, y: 2, z: 4, core: 2. Of those that a mesh axis runs over, the one named last changes fastest.
Arguments:
- acts: bfloat16 [1024, 8192], P(('dp', 'col'), 'row'), may hold values from -0.5 to 0.5
- grad_out: bfloat16 [1024, 14336], P(('dp', 'row'), 'col'), may hold values from -6 to 6
- weight: bfloat16 [8192, 14336], P('row', 'col'), may hold values from -0.0625 to 0.0625
Outputs:
- grad_input: bfloat16 [1024, 8192], P(('dp', 'col'), 'row')
- grad_weight: bfloat16 [4, 2048, 14336], P('row', 'dp', 'col')
All inputs are finite; a program needn't handle non-finite values.
Results may differ from a plain program's by a relative error of at most 0.001.
Values may be sent and summed in bfloat16 or wider, within the bound.
No kernel may reach another device: no remote copies, remote signals or barrier semaphores. Data moves between devices by JAX's collectives and lax.ppermute only.
A program may use at most 128 MiB of HBM per device.

v0:
```python
import jax
import jax.numpy as jnp
from jax import lax
from jax.sharding import PartitionSpec as P


def shards(acts, grad_out, weight):
    act_local = lax.all_gather(acts, "col", axis=0, tiled=True)
    partial_value = lax.dot_general(
        lax.all_gather(grad_out, "row", axis=0, tiled=True),
        weight,
        (((1,), (1,)), ((), ())),
        preferred_element_type=jnp.float32,
    )
    act_all = lax.all_to_all(act_local, "dp", split_axis=1, concat_axis=0, tiled=True)
    summed = lax.dot_general(
        act_all,
        lax.all_gather(grad_out, ("dp", "row"), axis=0, tiled=True),
        (((0,), (0,)), ((), ())),
        preferred_element_type=jnp.float32,
    )
    grad_weight = summed.astype(jnp.bfloat16)[None]
    grad_input = lax.psum_scatter(partial_value, "col", scatter_dimension=0, tiled=True).astype(
        jnp.bfloat16
    )
    return (grad_input, grad_weight)


def solution(mesh):
    in_specs = (P(("dp", "col"), "row"), P(("dp", "row"), "col"), P("row", "col"))
    out_specs = (P(("dp", "col"), "row"), P("row", "dp", "col"))
    return jax.shard_map(shards, mesh=mesh, in_specs=in_specs, out_specs=out_specs, check_vma=False)
```

profile of v0, /device:TPU:0, one launch (start us, length us, event | category | flops | bytes accessed | tf_op | source)
XLA Modules:
  0.0 239.2 jit_solution(466084870658492629)
XLA Ops:
  7.2 0.0 all-gather.4.cloned.1.call-start
  7.2 0.7 all-gather.4.cloned.1.call-update
  7.9 0.0 all-gather.6.cloned.1.call-start
  7.9 2.0 copy.5
  10.0 0.0 all-gather.6.cloned.1.call-update
  10.0 0.0 all-gather.8.cloned.1.call-start
  10.1 0.7 all-gather.8.cloned.1.call-update
  10.7 0.0 reduce-scatter.2.cloned.1.call-start
  10.8 33.0 %all-gather.4.cloned.1.call-done = bf16[512,3584]{1,0:T(8,128)(2,1)} async-done(((bf16[128,3584]{1,0:T(8,128)(2,1)}), bf16[512,3584]{1,0:T(8,128)(2,1)}) %all-gather.4.cloned.1.call-update) | async-done | bytes 3670032 | tf_op jit(solution)/shard_map/all_gather | solution.py:10
  43.8 13.4 %fusion.1 = f32[512,2048]{1,0:T(8,128)} fusion(bf16[512,3584]{1,0:T(8,128)(2,1)} %all-gather.4.cloned.1.call-done, bf16[2048,3584]{1,0:T(8,128)(2,1)} %param.5), kind=kOutput, calls=%fused_computation.2 | convolution fusion | flops 7516192768 | bytes 22544384 | tf_op jit(solution)/shard_map/dot_general | solution.py:9
  57.2 0.0 reduce-scatter.2.cloned.1.call-update
  57.2 35.0 %all-gather.6.cloned.1.call-done = bf16[512,2048]{0,1:T(8,128)(2,1)} async-done(((bf16[128,2048]{0,1:T(8,128)(2,1)}), bf16[512,2048]{0,1:T(8,128)(2,1)}) %all-gather.6.cloned.1.call-update) | async-done | bytes 2097168 | tf_op jit(solution)/shard_map/all_gather | solution.py:8
  92.2 39.6 %all_to_all.19 = bf16[512,2,1024]{0,2,1:T(8,128)(2,1)S(1)} all-to-all(bf16[512,2,1024]{0,2,1:T(8,128)(2,1)} %bitcast.10), channel_id=1, replica_groups=mesh['dp'=2,'row'=4,'col'=4] {'dp'}, dimensions={1} | all-to-all | bytes 4194304 | tf_op jit(solution)/shard_map/all_to_all | solution.py:15
  131.8 2.5 %copy.6 = bf16[2,512,1024]{2,1,0:T(8,128)(2,1)} copy(bf16[2,512,1024]{1,2,0:T(8,128)(2,1)S(1)} %bitcast.9) | data formatting | bytes 4194304 | tf_op jit(solution)/shard_map/all_to_all | solution.py:15
  134.3 17.7 %all-gather.8.cloned.1.call-done = bf16[1024,3584]{1,0:T(8,128)(2,1)} async-done(((bf16[128,3584]{1,0:T(8,128)(2,1)}), bf16[1024,3584]{1,0:T(8,128)(2,1)}) %all-gather.8.cloned.1.call-update) | async-done | bytes 7340048 | tf_op jit(solution)/shard_map/all_gather | solution.py:18
  151.9 12.6 %fusion = bf16[1,1024,3584]{2,1,0:T(8,128)(2,1)} fusion(bf16[1024,1024]{1,0:T(8,128)(2,1)} %bitcast.11, bf16[1024,3584]{1,0:T(8,128)(2,1)} %all-gather.8.cloned.1.call-done), kind=kOutput, calls=%fused_computation.1 | convolution fusion | flops 7519862784 | bytes 16777216 | tf_op jit(solution)/shard_map/dot_general | solution.py:16
  164.6 66.0 %reduce-scatter.2.cloned.1.call-done = f32[128,2048]{1,0:T(8,128)} async-done(((f32[512,2048]{1,0:T(8,128)}), f32[128,2048]{1,0:T(8,128)}) %reduce-scatter.2.cloned.1.call-update) | async-done | bytes 1048592 | tf_op jit(solution)/shard_map/reduce_scatter | solution.py:23
  230.6 2.1 convert_element_type.6
Async XLA Ops:
  7.2 36.6 %all-gather.4.cloned.1.call-start = ((), (), s32[]{:S(2)}) async-start(), calls=%async_computation.2 | async-start | bytes 4587520 | tf_op jit(solution)/shard_map/all_gather | solution.py:10
  7.9 84.3 %all-gather.6.cloned.1.call-start = ((), (), s32[]{:S(2)}) async-start(), calls=%async_computation.4 | async-start | bytes 2621440 | tf_op jit(solution)/shard_map/all_gather | solution.py:8
  10.0 141.9 %all-gather.8.cloned.1.call-start = ((), (), s32[]{:S(2)}) async-start(), calls=%async_computation.5 | async-start | bytes 8257536 | tf_op jit(solution)/shard_map/all_gather | solution.py:18
  10.7 219.8 %reduce-scatter.2.cloned.1.call-start = ((), (), s32[]{:S(2)}) async-start(), calls=%async_computation.3 | async-start | bytes 5242880 | tf_op jit(solution)/shard_map/reduce_scatter | solution.py:23
Sparse Core Ops, SparseCore 0:
  9.5 34.1 all-gather.3
  45.9 46.2 all-gather.5
  94.1 57.7 all-gather.7
  154.1 76.4 reduce-scatter.1
where the time goes:
time: 239 us
  waiting for transfers between devices  153 us (64%)
  blocking collectives  39.6 us (17%)
  matrix products  26 us (11%)
  between operations  13.8 us (6%)
  local copies, waits for them, and re-layouts  4.51 us (2%)
    reduce_scatter x1, waiting for transfers between devices, shards(): lax.psum_scatter(partial_value, 'col', scatter_dimension=0, tiled=True)  66 us
    all_to_all x1, blocking collectives, shards(): lax.all_to_all(act_local, 'dp', split_axis=1, concat_axis=0, tiled=True)  39.6 us
    all_gather x1, waiting for transfers between devices, shards(): act_local = lax.all_gather(acts, 'col', axis=0, tiled=True)  35 us
    all_gather x1, waiting for transfers between devices, shards(): lax.all_gather(grad_out, 'row', axis=0, tiled=True)  33 us
    all_gather x1, waiting for transfers between devices, shards(): lax.all_gather(grad_out, ('dp', 'row'), axis=0, tiled=True)  17.7 us
    dot_general x1, matrix products, shards(): lax.dot_general(lax.all_gather(grad_out, 'row', axis=0, tiled=True), weig...  13.4 us
    dot_general x1, matrix products, shards(): lax.dot_general(act_all, lax.all_gather(grad_out, ('dp', 'row'), axis=0,...  12.6 us
  transfers between devices with their start and end apart: 4, of which 4 were waited for; matrix products, arithmetic and copies ran while one was open for 13% of the time, Pallas kernels for 0%

commit v1 on v0

--- a/solution.py
+++ b/solution.py
@@ -2,6 +2,28 @@
 import jax.numpy as jnp
 from jax import lax
 from jax.sharding import PartitionSpec as P
+
+
+def laid_out(blocks, dim):
+    blocks = jnp.moveaxis(blocks, 0, dim)
+    lengths = blocks.shape
+    return blocks.reshape(*lengths[:dim], lengths[dim] * lengths[dim + 1], *lengths[dim + 2 :])
+
+
+def gather_around(x, axis, dim):
+    size = lax.axis_size(axis)
+    pairs = [(i, (i + 1) % size) for i in range(size)]
+    back = [(b, a) for a, b in pairs]
+    lower, upper = ([], [])
+    for turn in range(size - 1):
+        if turn % 2 == 0:
+            lower.append(lax.ppermute(lower[-1] if lower else x, axis, pairs))
+        else:
+            upper.append(lax.ppermute(upper[-1] if upper else x, axis, back))
+    blocks = jnp.stack([*lower[::-1], x, *upper])
+    shift = lax.axis_index(axis) - len(lower)
+    blocks = blocks[(jnp.arange(size) - shift) % size]
+    return laid_out(blocks, dim)
 
 
 def shards(acts, grad_out, weight):
@@ -15,7 +37,7 @@
     act_all = lax.all_to_all(act_local, "dp", split_axis=1, concat_axis=0, tiled=True)
     summed = lax.dot_general(
         act_all,
-        lax.all_gather(grad_out, ("dp", "row"), axis=0, tiled=True),
+        gather_around(grad_out, ("dp", "row"), 0),
         (((0,), (0,)), ((), ())),
         preferred_element_type=jnp.float32,
     )

time: 239 us -> 212 us (0.89)
  waiting for transfers between devices: 153 us -> 86.6 us
  starting transfers between devices: 0.16 us -> 44.5 us
  blocking collectives: 39.6 us -> 0 us
  local copies, waits for them, and re-layouts: 4.51 us -> 37.9 us
    ppermute x0 -> x7, starting transfers between devices: none -> 40.6 us  [the longest x4 37.9 us: gather_around(): lower.append(lax.ppermute(lower[-1] if lower else x, axis, pairs))]
    all_to_all x1 -> x0, blocking collectives: 39.6 us -> none  [shards(): lax.all_to_all(act_local, 'dp', split_axis=1, concat_axis=0, tiled=True)]
    all_gather x1, waiting for transfers between devices: 35 us -> 0.02 us  [shards(): act_local = lax.all_gather(acts, 'col', axis=0, tiled=True)]
    ppermute x0 -> x7, waiting for transfers between devices: none -> 31.3 us  [the longest x4 31.2 us: gather_around(): lower.append(lax.ppermute(lower[-1] if lower else x, axis, pairs))]
    reduce_scatter x1, waiting for transfers between devices: 66 us -> 38.6 us  [shards(): lax.psum_scatter(partial_value, 'col', scatter_dimension=0, tiled=True)]
    unnamed x1 -> x21, local copies, waits for them, and re-layouts: 2.04 us -> 25.9 us
    all_gather x1 -> x0, waiting for transfers between devices: 17.7 us -> none  [shards(): lax.all_gather(grad_out, ('dp', 'row'), axis=0, tiled=True)]
    all_gather x1, waiting for transfers between devices: 33 us -> 15.9 us  [shards(): lax.all_gather(grad_out, 'row', axis=0, tiled=True)]
  transfers between devices with their start and end apart: 4 -> 11, of which waited for: 4 -> 5; matrix products, arithmetic and copies ran while one was open for 13% -> 29% of each run, Pallas kernels for 0% -> 0%
where the time goes in v1:
time: 212 us; the launch traced here: 211 us
  waiting for transfers between devices  86.6 us (41%)
  starting transfers between devices  44.5 us (21%)
  local copies, waits for them, and re-layouts  37.9 us (18%)
  matrix products  26 us (12%)
  between operations  13.8 us (7%)
    reduce_scatter x1, waiting for transfers between devices, shards(): lax.psum_scatter(partial_value, 'col', scatter_dimension=0, tiled=True)  38.6 us
    ppermute x4, starting transfers between devices, gather_around(): lower.append(lax.ppermute(lower[-1] if lower else x, axis, pairs))  37.9 us
    ppermute x4, waiting for transfers between devices, gather_around(): lower.append(lax.ppermute(lower[-1] if lower else x, axis, pairs))  31.2 us
    unnamed x21, local copies, waits for them, and re-layouts  25.9 us
    all_gather x1, waiting for transfers between devices, shards(): lax.all_gather(grad_out, 'row', axis=0, tiled=True)  15.9 us
    dot_general x1, matrix products, shards(): lax.dot_general(lax.all_gather(grad_out, 'row', axis=0, tiled=True), weig...  13.4 us
    dot_general x1, matrix products, shards(): lax.dot_general(act_all, gather_around(grad_out, ('dp', 'row'), 0), (((0,...  12.7 us
    gather x1, local copies, waits for them, and re-layouts, gather_around(): blocks = blocks[(jnp.arange(size) - shift) % size]  7.45 us
  transfers between devices with their start and end apart: 11, of which 5 were waited for; matrix products, arithmetic and copies ran while one was open for 29% of the time, Pallas kernels for 0%

profile of v1, /device:TPU:0, one launch (start us, length us, event | category | flops | bytes accessed | tf_op | source)
XLA Modules:
  0.0 210.9 jit_solution(14790507804208361491)
XLA Ops:
  7.2 2.0 copy.7
  10.6 14.2 %collective-permute-done = bf16[128,3584]{1,0:T(8,128)(2,1)S(1)} collective-permute-done((bf16[128,3584]{1,0:T(8,128)(2,1)}, bf16[128,3584]{1,0:T(8,128)(2,1)S(1)}, u32[]{:S(2)}, u32[]{:S(2)}) %collective-permute-start) | collective-permute-done | bytes 917536 | tf_op jit(solution)/shard_map/ppermute | solution.py:20
  25.7 2.6 %collective-permute-start.4 = (bf16[128,3584]{1,0:T(8,128)(2,1)}, bf16[128,3584]{1,0:T(8,128)(2,1)S(1)}, u32[]{:S(2)}, u32[]{:S(2)}) collective-permute-start(bf16[128,3584]{1,0:T(8,128)(2,1)} %param.4), channel_id=1, source_target_pairs={{4,0},{8,4},{12,8},{16,12},{20,16},{24,20},{28,24},{0,28},{5,1},{9... | collective-permute-start | bytes 2752520 | tf_op jit(solution)/shard_map/ppermute | solution.py:22
  28.3 11.2 %collective-permute-done.1 = bf16[128,3584]{1,0:T(8,128)(2,1)S(1)} collective-permute-done((bf16[128,3584]{1,0:T(8,128)(2,1)S(1)}, bf16[128,3584]{1,0:T(8,128)(2,1)S(1)}, u32[]{:S(2)}, u32[]{:S(2)}) %collective-permute-start.1) | collective-permute-done | bytes 917536 | tf_op jit(solution)/shard_map/ppermute | solution.py:20
  39.5 7.8 %collective-permute-start.2 = (bf16[128,3584]{1,0:T(8,128)(2,1)S(1)}, bf16[128,3584]{1,0:T(8,128)(2,1)S(1)}, u32[]{:S(2)}, u32[]{:S(2)}) collective-permute-start(bf16[128,3584]{1,0:T(8,128)(2,1)S(1)} %collective-permute-done.1), channel_id=1, source_target_pairs={{0,4},{4,8},{8,12},{12,16},{16,20},{20,24},{24,28},{28,0},{1,5},{5... | collective-permute-start | bytes 2752520 | tf_op jit(solution)/shard_map/ppermute | solution.py:20
  47.4 5.9 %collective-permute-done.2 = bf16[128,3584]{1,0:T(8,128)(2,1)S(1)} collective-permute-done((bf16[128,3584]{1,0:T(8,128)(2,1)S(1)}, bf16[128,3584]{1,0:T(8,128)(2,1)S(1)}, u32[]{:S(2)}, u32[]{:S(2)}) %collective-permute-start.2) | collective-permute-done | bytes 917536 | tf_op jit(solution)/shard_map/ppermute | solution.py:20
  53.3 29.5 %collective-permute-start.3 = (bf16[128,3584]{1,0:T(8,128)(2,1)S(1)}, bf16[128,3584]{1,0:T(8,128)(2,1)}, u32[]{:S(2)}, u32[]{:S(2)}) collective-permute-start(bf16[128,3584]{1,0:T(8,128)(2,1)S(1)} %collective-permute-done.2), channel_id=1, source_target_pairs={{0,4},{4,8},{8,12},{12,16},{16,20},{20,24},{24,28},{28,0},{1,5},{5... | collective-permute-start | bytes 2752520 | tf_op jit(solution)/shard_map/ppermute | solution.py:20
  82.9 3.8 %all-to-all-start = ((bf16[512,2,1024]{0,2,1:T(8,128)(2,1)}), bf16[512,2,1024]{0,2,1:T(8,128)(2,1)S(1)}, u32[]{:S(2)}, u32[]{:S(2)}) async-start(bf16[512,2,1024]{0,2,1:T(8,128)(2,1)} %bitcast.32), calls=%async_computation.1 | async-start | bytes 4194304 | tf_op jit(solution)/shard_map/all_to_all | solution.py:37
  86.8 2.2 %bitcast_dynamic-update-slice_fusion.7 = bf16[8,128,3584]{2,1,0:T(8,128)(2,1)} fusion(bf16[128,3584]{1,0:T(8,128)(2,1)} %collective-permute-done.3), kind=kLoop, calls=%fused_computation.10 | loop fusion | bytes 1835008
  89.0 15.9 %all-gather.3.cloned.1.call-done = bf16[512,3584]{1,0:T(8,128)(2,1)} async-done(((bf16[128,3584]{1,0:T(8,128)(2,1)}), bf16[512,3584]{1,0:T(8,128)(2,1)}) %all-gather.3.cloned.1.call-update) | async-done | bytes 3670032 | tf_op jit(solution)/shard_map/all_gather | solution.py:32
  104.9 13.4 %fusion.3 = f32[512,2048]{1,0:T(8,128)} fusion(bf16[512,3584]{1,0:T(8,128)(2,1)} %all-gather.3.cloned.1.call-done, bf16[2048,3584]{1,0:T(8,128)(2,1)} %param.5), kind=kOutput, calls=%fused_computation.18 | convolution fusion | flops 7516192768 | bytes 22544384 | tf_op jit(solution)/shard_map/dot_general | solution.py:31
  118.3 2.3 %bitcast_dynamic-update-slice_fusion.6 = bf16[8,128,3584]{2,1,0:T(8,128)(2,1)} fusion(bf16[8,128,3584]{2,1,0:T(8,128)(2,1)} %bitcast_dynamic-update-slice_fusion.7, bf16[128,3584]{1,0:T(8,128)(2,1)} %copy-done.5), kind=kLoop, calls=%fused_computation.9 | loop fusion | bytes 1835008
  120.6 2.2 %bitcast_dynamic-update-slice_fusion.5 = bf16[8,128,3584]{2,1,0:T(8,128)(2,1)} fusion(bf16[8,128,3584]{2,1,0:T(8,128)(2,1)} %bitcast_dynamic-update-slice_fusion.6, bf16[128,3584]{1,0:T(8,128)(2,1)} %copy-done.4), kind=kLoop, calls=%fused_computation.8 | loop fusion | bytes 1835008
  122.8 2.2 %bitcast_dynamic-update-slice_fusion.4 = bf16[8,128,3584]{2,1,0:T(8,128)(2,1)} fusion(bf16[8,128,3584]{2,1,0:T(8,128)(2,1)} %bitcast_dynamic-update-slice_fusion.5, bf16[128,3584]{1,0:T(8,128)(2,1)} %copy-done.1), kind=kLoop, calls=%fused_computation.7 | loop fusion | bytes 1835008
  124.9 1.0 bitcast_dynamic-update-slice_fusion.3
  125.9 1.0 bitcast_dynamic-update-slice_fusion.2
  126.9 2.2 %bitcast_dynamic-update-slice_fusion.1 = bf16[8,128,3584]{2,1,0:T(8,128)(2,1)} fusion(bf16[8,128,3584]{2,1,0:T(8,128)(2,1)} %bitcast_dynamic-update-slice_fusion.2, bf16[128,3584]{1,0:T(8,128)(2,1)} %collective-permute-done.5), kind=kLoop, calls=%fused_computation.4 | loop fusion | bytes 1835008
  129.1 2.2 %bitcast_dynamic-update-slice_fusion = bf16[8,128,3584]{2,1,0:T(8,128)(2,1)} fusion(bf16[8,128,3584]{2,1,0:T(8,128)(2,1)} %bitcast_dynamic-update-slice_fusion.1, bf16[128,3584]{1,0:T(8,128)(2,1)} %collective-permute-done.6), kind=kLoop, calls=%fused_computation.3 | loop fusion | bytes 1835008 | tf_op jit(solution)/shard_map/stack | solution.py:23
  131.2 7.5 %gather_fusion = bf16[8,128,3584]{2,1,0:T(8,128)(2,1)} fusion(bf16[8,128,3584]{2,1,0:T(8,128)(2,1)} %bitcast_dynamic-update-slice_fusion, s32[1024]{0:T(1024)S(1)} %pad_clamp_fusion), kind=kCustom, calls=%fused_computation | custom fusion | bytes 14680096 | tf_op jit(solution)/shard_map/gather | solution.py:25
  138.7 2.4 %copy.8 = bf16[2,512,1024]{2,1,0:T(8,128)(2,1)} copy(bf16[2,512,1024]{1,2,0:T(8,128)(2,1)S(1)} %bitcast.30) | data formatting | bytes 4194304 | tf_op jit(solution)/shard_map/all_to_all | solution.py:37
  141.0 12.7 %fusion = bf16[1,1024,3584]{1,2,0:T(8,128)(2,1)} fusion(bf16[1024,3584]{1,0:T(8,128)(2,1)} %bitcast.31, bf16[1024,1024]{1,0:T(8,128)(2,1)} %bitcast.33), kind=kOutput, calls=%fused_computation.2 | convolution fusion | flops 7519862784 | bytes 16777216 | tf_op jit(solution)/shard_map/dot_general | solution.py:38
  153.7 10.0 %copy.9 = bf16[1,1024,3584]{2,1,0:T(8,128)(2,1)} copy(bf16[1,1024,3584]{1,2,0:T(8,128)(2,1)} %fusion) | data formatting | bytes 14680064
  163.7 38.6 %reduce-scatter.2.cloned.1.call-done = f32[128,2048]{1,0:T(8,128)} async-done(((f32[512,2048]{1,0:T(8,128)}), f32[128,2048]{1,0:T(8,128)}) %reduce-scatter.2.cloned.1.call-update) | async-done | bytes 1048592 | tf_op jit(solution)/shard_map/reduce_scatter | solution.py:45
  202.3 2.1 convert_element_type.9
  (30 shorter events, 2.5 us)
Async XLA Ops:
  7.2 75.8 %all-gather.5.cloned.1.call-start = ((), (), s32[]{:S(2)}) async-start(), calls=%async_computation.4 | async-start | bytes 2621440 | tf_op jit(solution)/shard_map/all_gather | solution.py:30
  9.3 95.6 %all-gather.3.cloned.1.call-start = ((), (), s32[]{:S(2)}) async-start(), calls=%async_computation.2 | async-start | bytes 4587520 | tf_op jit(solution)/shard_map/all_gather | solution.py:32
  10.0 14.7 %collective-permute-start = (bf16[128,3584]{1,0:T(8,128)(2,1)}, bf16[128,3584]{1,0:T(8,128)(2,1)S(1)}, u32[]{:S(2)}, u32[]{:S(2)}) collective-permute-start(bf16[128,3584]{1,0:T(8,128)(2,1)} %param.4), channel_id=1, source_target_pairs={{0,4},{4,8},{8,12},{12,16},{16,20},{20,24},{24,28},{28,0},{1,5},{5... | collective-permute-start | bytes 2752520 | tf_op jit(solution)/shard_map/ppermute | solution.py:20
  24.7 0.9 copy-start.1
  25.7 13.8 %collective-permute-start.1 = (bf16[128,3584]{1,0:T(8,128)(2,1)S(1)}, bf16[128,3584]{1,0:T(8,128)(2,1)S(1)}, u32[]{:S(2)}, u32[]{:S(2)}) collective-permute-start(bf16[128,3584]{1,0:T(8,128)(2,1)S(1)} %collective-permute-done), channel_id=1, source_target_pairs={{0,4},{4,8},{8,12},{12,16},{16,20},{20,24},{24,28},{28,0},{1,5},{5... | collective-permute-start | bytes 2752520 | tf_op jit(solution)/shard_map/ppermute | solution.py:20
  25.7 21.7 %collective-permute-start.4 = (bf16[128,3584]{1,0:T(8,128)(2,1)}, bf16[128,3584]{1,0:T(8,128)(2,1)S(1)}, u32[]{:S(2)}, u32[]{:S(2)}) collective-permute-start(bf16[128,3584]{1,0:T(8,128)(2,1)} %param.4), channel_id=1, source_target_pairs={{4,0},{8,4},{12,8},{16,12},{20,16},{24,20},{28,24},{0,28},{5,1},{9... | collective-permute-start | bytes 2752520 | tf_op jit(solution)/shard_map/ppermute | solution.py:22
  39.5 7.8 %copy-start.4 = (bf16[128,3584]{1,0:T(8,128)(2,1)}, bf16[128,3584]{1,0:T(8,128)(2,1)S(1)}, u32[]{:S(2)}) copy-start(bf16[128,3584]{1,0:T(8,128)(2,1)S(1)} %collective-permute-done.1) | copy-start | bytes 2752516
  39.5 13.8 %collective-permute-start.2 = (bf16[128,3584]{1,0:T(8,128)(2,1)S(1)}, bf16[128,3584]{1,0:T(8,128)(2,1)S(1)}, u32[]{:S(2)}, u32[]{:S(2)}) collective-permute-start(bf16[128,3584]{1,0:T(8,128)(2,1)S(1)} %collective-permute-done.1), channel_id=1, source_target_pairs={{0,4},{4,8},{8,12},{12,16},{16,20},{20,24},{24,28},{28,0},{1,5},{5... | collective-permute-start | bytes 2752520 | tf_op jit(solution)/shard_map/ppermute | solution.py:20
  47.3 35.6 %copy-start.2 = (bf16[128,3584]{1,0:T(8,128)(2,1)}, bf16[128,3584]{1,0:T(8,128)(2,1)S(1)}, u32[]{:S(2)}) copy-start(bf16[128,3584]{1,0:T(8,128)(2,1)S(1)} %collective-permute-done.4) | copy-start | bytes 2752516
  47.3 35.5 %collective-permute-start.5 = (bf16[128,3584]{1,0:T(8,128)(2,1)S(1)}, bf16[128,3584]{1,0:T(8,128)(2,1)}, u32[]{:S(2)}, u32[]{:S(2)}) collective-permute-start(bf16[128,3584]{1,0:T(8,128)(2,1)S(1)} %collective-permute-done.4), channel_id=1, source_target_pairs={{4,0},{8,4},{12,8},{16,12},{20,16},{24,20},{28,24},{0,28},{5,1},{9... | collective-permute-start | bytes 2752520 | tf_op jit(solution)/shard_map/ppermute | solution.py:22
  53.3 51.6 %copy-start.5 = (bf16[128,3584]{1,0:T(8,128)(2,1)}, bf16[128,3584]{1,0:T(8,128)(2,1)S(1)}, u32[]{:S(2)}) copy-start(bf16[128,3584]{1,0:T(8,128)(2,1)S(1)} %collective-permute-done.2) | copy-start | bytes 2752516
  53.3 33.5 %collective-permute-start.3 = (bf16[128,3584]{1,0:T(8,128)(2,1)S(1)}, bf16[128,3584]{1,0:T(8,128)(2,1)}, u32[]{:S(2)}, u32[]{:S(2)}) collective-permute-start(bf16[128,3584]{1,0:T(8,128)(2,1)S(1)} %collective-permute-done.2), channel_id=1, source_target_pairs={{0,4},{4,8},{8,12},{12,16},{16,20},{20,24},{24,28},{28,0},{1,5},{5... | collective-permute-start | bytes 2752520 | tf_op jit(solution)/shard_map/ppermute | solution.py:20
  82.8 46.2 %collective-permute-start.6 = (bf16[128,3584]{1,0:T(8,128)(2,1)}, bf16[128,3584]{1,0:T(8,128)(2,1)}, u32[]{:S(2)}, u32[]{:S(2)}) collective-permute-start(bf16[128,3584]{1,0:T(8,128)(2,1)} %collective-permute-done.5), channel_id=1, source_target_pairs={{4,0},{8,4},{12,8},{16,12},{20,16},{24,20},{28,24},{0,28},{5,1},{9... | collective-permute-start | bytes 2752520 | tf_op jit(solution)/shard_map/ppermute | solution.py:22
  82.9 55.7 %all-to-all-start = ((bf16[512,2,1024]{0,2,1:T(8,128)(2,1)}), bf16[512,2,1024]{0,2,1:T(8,128)(2,1)S(1)}, u32[]{:S(2)}, u32[]{:S(2)}) async-start(bf16[512,2,1024]{0,2,1:T(8,128)(2,1)} %bitcast.32), calls=%async_computation.1 | async-start | bytes 4194304 | tf_op jit(solution)/shard_map/all_to_all | solution.py:37
  86.7 115.6 %reduce-scatter.2.cloned.1.call-start = ((), (), s32[]{:S(2)}) async-start(), calls=%async_computation.3 | async-start | bytes 5242880 | tf_op jit(solution)/shard_map/reduce_scatter | solution.py:45
  118.3 6.7 %copy-start = (bf16[128,3584]{1,0:T(8,128)(2,1)S(1)}, bf16[128,3584]{1,0:T(8,128)(2,1)}, u32[]{:S(2)}) copy-start(bf16[128,3584]{1,0:T(8,128)(2,1)} %param.4) | copy-start | bytes 2752516
  118.3 7.6 %copy-start.3 = (bf16[128,3584]{1,0:T(8,128)(2,1)S(1)}, bf16[128,3584]{1,0:T(8,128)(2,1)}, u32[]{:S(2)}) copy-start(bf16[128,3584]{1,0:T(8,128)(2,1)} %copy-done.2) | copy-start | bytes 2752516
Sparse Core Ops, SparseCore 0:
  10.1 48.9 all-gather.4
  60.7 44.1 all-gather.2
  118.4 83.8 reduce-scatter.1
